TPU v7x, 32 devices: a whole 2x2x4 slice. The times are simulated.
32 devices in a mesh: gx: 4 (over x, core), gy: 4 (over z), gz: 2 (over y).
Axes of the slice: x: 2, y: 2, z: 4, core: 2. Of those that a mesh axis runs over, the one named last changes fastest.
Arguments:
- loads: bfloat16 [4, 4, 2, 2048, 128], P('gx', 'gy', 'gz'), may hold values from -12 to 12, as said below
- start_guess: bfloat16 [4, 4, 2, 2048, 128], P('gx', 'gy', 'gz'), may hold values from -1.1953125 to 1.1953125
- schur_blocks: bfloat16 [4, 4, 2, 2048, 2048], P('gx', 'gy', 'gz'), may hold values from -1 to 5, as said below
- coupling: bfloat16 [4, 4, 2, 6, 128, 128], P('gx', 'gy', 'gz'), may hold values from -0.25 to 0.25
- diag_inverse: bfloat16 [4, 4, 2, 16, 128, 128], P('gx', 'gy', 'gz'), may hold values from -1 to 1, as said below
- lower_blocks: bfloat16 [4, 4, 2, 15, 128, 128], P('gx', 'gy', 'gz'), may hold values from -0.1875 to 0.1875
- upper_blocks: bfloat16 [4, 4, 2, 15, 128, 128], P('gx', 'gy', 'gz'), may hold values from -0.1875 to 0.1875
Outputs:
- solution: float32 [4, 4, 2, 2048, 128], P('gx', 'gy', 'gz')
- residual_ratio: float32 [128], replicated
Inputs may be any that keep to these rules, and one draw needn't show every extreme that they name: Each subdomain's loads are independent entries times a factor of that subdomain. `schur_blocks`: each subdomain's Schur block has a positive diagonal between 2 and 4 and full independent off-diagonal entries. `diag_inverse`: each block has a positive diagonal between 0.25 and 0.5 and full independent off-diagonal entries.
All inputs are finite; a program needn't handle non-finite values.
Results may differ from a plain program's by a relative error of at most 0.0037.
Values may be sent and summed in bfloat16 or wider, within the bound.
A program may use at most 64 MiB of HBM per device.

v0:
```python
import jax
import jax.numpy as jnp
from jax import lax
from jax.sharding import PartitionSpec as P

U = 2048
F = 128
B = 128
R = 128
ITERS = 2
NB = 16
epsilon = 1e-06


def with_halo(cells, sides, width):
    for axis, dim in sides:
        count = lax.axis_size(axis)
        head = lax.slice_in_dim(cells, 0, width, axis=dim)
        tail = lax.slice_in_dim(cells, cells.shape[dim] - width, cells.shape[dim], axis=dim)
        cells = jnp.concatenate(
            [
                lax.ppermute(tail, axis, [(i, (i + 1) % count) for i in range(count)]),
                cells,
                lax.ppermute(head, axis, [((i + 1) % count, i) for i in range(count)]),
            ],
            axis=dim,
        )
    return cells


def neighbour_faces(face_rows):
    along_x = with_halo(face_rows[0:2][None], (("gx", 0),), 1)
    along_y = with_halo(face_rows[2:4][None], (("gy", 0),), 1)
    along_z = with_halo(face_rows[4:6][None], (("gz", 0),), 1)
    return jnp.stack(
        [along_x[0, 1], along_x[2, 0], along_y[0, 1], along_y[2, 0], along_z[0, 1], along_z[2, 0]]
    )


def operate(values, schur_block, couple_block):
    own_part = jnp.dot(schur_block, values, preferred_element_type=jnp.float32)
    face_rows = values[: 6 * F].reshape(6, F, values.shape[1])
    neighbours = neighbour_faces(face_rows)
    coupled = lax.dot_general(
        couple_block, neighbours, (((2,), (1,)), ((0,), (0,))), preferred_element_type=jnp.float32
    )
    return jnp.concatenate(
        [own_part[: 6 * F] + coupled.reshape(6 * F, R), own_part[6 * F :]], axis=0
    )


def precondition(values, diag_blocks, lower_one, upper_one):
    blocks = values.reshape(NB, B, R)

    def forward(previous, inputs):
        block_in, lower_block = inputs
        current = block_in - jnp.dot(
            lower_block, previous.astype(jnp.bfloat16), preferred_element_type=jnp.float32
        )
        return (current, current)

    carried, remaining = lax.scan(forward, blocks[0], (blocks[1:], lower_one))
    forward_sweep = jnp.concatenate([blocks[0][None], remaining], axis=0)
    final_block = jnp.dot(
        diag_blocks[NB - 1],
        forward_sweep[NB - 1].astype(jnp.bfloat16),
        preferred_element_type=jnp.float32,
    )

    def backward(next_block, inputs):
        block_in, diag_block, upper_block = inputs
        inner = block_in - jnp.dot(
            upper_block, next_block.astype(jnp.bfloat16), preferred_element_type=jnp.float32
        )
        current = jnp.dot(
            diag_block, inner.astype(jnp.bfloat16), preferred_element_type=jnp.float32
        )
        return (current, current)

    carried, earlier = lax.scan(
        backward, final_block, (forward_sweep[:-1], diag_blocks[:-1], upper_one), reverse=True
    )
    return jnp.concatenate([earlier, final_block[None]], axis=0).reshape(U, R)


def least_squares(hessenberg, start_norm):
    columns = hessenberg.shape[1]
    unit_vectors = []
    triangle = {}
    for column in range(columns):
        vector = hessenberg[:, column]
        for earlier in range(column):
            weight = jnp.sum(unit_vectors[earlier] * vector, axis=0)
            triangle[earlier, column] = weight
            vector = vector - weight * unit_vectors[earlier]
        length = jnp.sqrt(jnp.sum(vector * vector, axis=0))
        triangle[column, column] = length
        unit_vectors.append(vector / length)
    target = [start_norm * unit_vectors[column][0] for column in range(columns)]
    coeffs = [None] * columns
    for column in range(columns - 1, -1, -1):
        running = target[column]
        for earlier in range(column + 1, columns):
            running = running - triangle[column, earlier] * coeffs[earlier]
        coeffs[column] = running / triangle[column, column]
    coeffs = jnp.stack(coeffs)
    unit_first = jnp.zeros((columns + 1, 1), jnp.float32).at[0].set(1.0)
    misfit = unit_first * start_norm - jnp.sum(hessenberg * coeffs[None], axis=1)
    return (coeffs, jnp.sqrt(jnp.sum(misfit * misfit, axis=0)) / start_norm)


def body(loads, start_guess, schur_blocks, coupling, diag_inverse, lower_blocks, upper_blocks):
    schur_block = schur_blocks[0, 0, 0]
    couple_block = coupling[0, 0, 0]
    diag_blocks = diag_inverse[0, 0, 0]
    lower_one = lower_blocks[0, 0, 0]
    upper_one = upper_blocks[0, 0, 0]
    warm_start = start_guess[0, 0, 0]
    residual = loads[0, 0, 0].astype(jnp.float32) - operate(warm_start, schur_block, couple_block)
    start_norm = jnp.sqrt(
        lax.psum(jnp.sum(residual * residual, axis=0), ("gx", "gy", "gz")) + epsilon
    )
    krylov = [residual / start_norm]
    hessenberg = jnp.zeros((ITERS + 1, ITERS, R), jnp.float32)
    directions = []
    for column in range(ITERS):
        direction = precondition(krylov[column], diag_blocks, lower_one, upper_one)
        directions.append(direction)
        mapped = operate(direction.astype(jnp.bfloat16), schur_block, couple_block)
        stacked = jnp.stack(krylov)
        own_products = jnp.sum(stacked * mapped[None], axis=1)
        projected, squares = lax.psum(
            (own_products, jnp.sum(mapped * mapped, axis=0)), ("gx", "gy", "gz")
        )
        mapped = mapped - jnp.sum(projected[:, None, :] * stacked, axis=0)
        length = jnp.sqrt(squares - jnp.sum(projected * projected, axis=0) + epsilon)
        hessenberg = (
            hessenberg.at[: column + 1, column].set(projected).at[column + 1, column].set(length)
        )
        if column + 1 < ITERS:
            krylov.append(mapped / length)
    coeffs, residual_ratio = least_squares(hessenberg, start_norm)
    solution = warm_start.astype(jnp.float32)
    for column in range(ITERS):
        solution = solution + coeffs[column] * directions[column]
    return (solution[None, None, None], residual_ratio)


def solution(mesh):
    in_specs = (
        P("gx", "gy", "gz", None, None),
        P("gx", "gy", "gz", None, None),
        P("gx", "gy", "gz", None, None),
        P("gx", "gy", "gz", None, None, None),
        P("gx", "gy", "gz", None, None, None),
        P("gx", "gy", "gz", None, None, None),
        P("gx", "gy", "gz", None, None, None),
    )
    out_specs = (P("gx", "gy", "gz", None, None), P())
    return jax.shard_map(body, mesh=mesh, in_specs=in_specs, out_specs=out_specs, check_vma=False)
```

profile of v0, /device:TPU:0, one launch (start us, length us, event | category | flops | bytes accessed | tf_op | source)
XLA Modules:
  0.0 269.4 jit_solution(9059985981006871884)
XLA Ops:
  2.2 2.0 collective-permute-start.1
  4.2 2.3 collective-permute-start.2
  6.5 2.0 collective-permute-start.3
  8.6 1.7 collective-permute-start.4
  10.3 5.8 %fusion.40 = f32[2048,128]{1,0:T(8,128)S(1)} fusion(bf16[1,1,1,2048,2048]{4,3,2,1,0:T(8,128)(2,1)} %param.27, bf16[1,1,1,2048,128]{4,3,2,1,0:T(8,128)(2,1)} %param.26), kind=kOutput, calls=%fused_computation.40 | convolution fusion | flops 1073741824 | bytes 9961472 | tf_op jit(solution)/shard_map/dot_general | solution.py:41
  18.9 3.9 %collective-permute-done.5 = bf16[1,2,128,128]{3,2,1,0:T(8,128)(2,1)S(1)} collective-permute-done((bf16[1,2,128,128]{3,2,1,0:T(8,128)(2,1)S(1)}, bf16[1,2,128,128]{3,2,1,0:T(8,128)(2,1)S(1)}, u32[]{:S(2)}, u32[]{:S(2)}) %collective-permute-start.5) | collective-permute-done | bytes 65568 | tf_op jit(solution)/shard_map/ppermute | solution.py:24
  23.4 37.7 %psum.35 = f32[128]{0:T(128)S(1)} all-reduce(f32[128]{0:T(128)S(1)} %multiply_reduce_fusion.3), channel_id=1, replica_groups=mesh['gx'=4,'gy'=4,'gz'=2] {'gx','gy','gz'}, use_global_device_ids=true, to_apply=%region_1.0 | all-reduce | flops 128 | bytes 1024 | tf_op jit(solution)/shard_map/psum | solution.py:121
  61.1 1.2 fusion.52
  63.4 15.6 %while.61 = (s32[]{:T(128)}, bf16[128,128]{1,0:T(8,128)(2,1)S(1)}, f32[15,128,128]{2,1,0:T(8,128)S(1)}, f32[15,128,128]{2,1,0:T(8,128)}, bf16[15,128,128]{2,1,0:T(8,128)(2,1)}, /*index=5*/s32[]{:T(128)}) while((s32[]{:T(128)}, bf16[128,128]{1,0:T(8,128)(2,1)S(1)}, f32[15,128,128]{2,1,0:T(8,128)S(1)}, f32[15,128,128]{2,1,0:T(8,128)}, ...), condition=%wide.region_3.4_spmd, body=%wide.region_2.3_spmd.sunk | while | flops 4227074 | bytes 296005 | solution.py:62
  81.0 18.0 %while.62 = (s32[]{:T(128)}, bf16[128,128]{1,0:T(8,128)(2,1)S(1)}, f32[15,128,128]{2,1,0:T(8,128)S(1)}, bf16[15,128,128]{2,1,0:T(8,128)(2,1)}, f32[15,128,128]{2...) while((s32[]{:T(128)}, bf16[128,128]{1,0:T(8,128)(2,1)S(1)}, ...), condition=%wide.region_5.6_spmd, body=%wide.region_4.5_spmd.sunk | while | flops 8437763 | bytes 329825 | solution.py:80
  81.0 1.2 bitcast_dynamic-update-slice_fusion.9
  82.2 1.2 bitcast_dynamic-update-slice_fusion.9
  83.4 1.2 bitcast_dynamic-update-slice_fusion.9
  84.6 1.2 bitcast_dynamic-update-slice_fusion.9
  85.8 1.2 bitcast_dynamic-update-slice_fusion.9
  87.0 1.2 bitcast_dynamic-update-slice_fusion.9
  88.2 1.2 bitcast_dynamic-update-slice_fusion.9
  89.4 1.2 bitcast_dynamic-update-slice_fusion.9
  90.6 1.2 bitcast_dynamic-update-slice_fusion.9
  91.8 1.2 bitcast_dynamic-update-slice_fusion.9
  93.0 1.2 bitcast_dynamic-update-slice_fusion.9
  94.2 1.2 bitcast_dynamic-update-slice_fusion.9
  95.4 1.2 bitcast_dynamic-update-slice_fusion.9
  96.6 1.2 bitcast_dynamic-update-slice_fusion.9
  97.8 1.2 bitcast_dynamic-update-slice_fusion.9
  99.1 1.7 collective-permute-start.7
  100.9 2.0 collective-permute-start.8
  102.8 1.9 collective-permute-start.9
  104.7 5.9 %fusion.42 = f32[2048,128]{1,0:T(8,128)S(1)} fusion(bf16[2048,128]{1,0:T(8,128)(2,1)S(1)} %bitcast.335, bf16[1,1,1,2048,2048]{4,3,2,1,0:T(8,128)(2,1)} %param.27), kind=kOutput, calls=%fused_computation.42 | convolution fusion | flops 1073741824 | bytes 9961472 | tf_op jit(solution)/shard_map/dot_general | solution.py:41
  111.8 2.3 collective-permute-start.10
  114.2 2.8 %collective-permute-done.10 = bf16[1,2,128,128]{3,2,1,0:T(8,128)(2,1)S(1)} collective-permute-done((bf16[1,2,128,128]{3,2,1,0:T(8,128)(2,1)S(1)}, bf16[1,2,128,128]{3,2,1,0:T(8,128)(2,1)S(1)}, u32[]{:S(2)}, u32[]{:S(2)}) %collective-permute-start.10) | collective-permute-done | bytes 65568 | tf_op jit(solution)/shard_map/ppermute | solution.py:22
  116.9 1.4 collective-permute-done.11
  119.2 38.1 %all-reduce.2 = (f32[128]{0:T(128)S(1)}, f32[1,128]{1,0:T(1,128)S(1)}) all-reduce(f32[128]{0:T(128)S(1)} %multiply_reduce_fusion.1, f32[1,128]{1,0:T(1,128)S(1)} %bitcast.351), channel_id=1, replica_groups=mesh['gx'=4,'gy'=4,'gz'=2] {'gx','gy','gz'}, use_global_device_ids=true, to_apply=%region_9.10 | all-reduce | flops 256 | bytes 2048 | tf_op jit(solution)/shard_map/psum | solution.py:132
  157.3 1.3 subtract_divide_fusion
  159.7 15.6 %while.63 = (s32[]{:T(128)}, bf16[128,128]{1,0:T(8,128)(2,1)S(1)}, f32[15,128,128]{2,1,0:T(8,128)S(1)}, f32[15,128,128]{2,1,0:T(8,128)}, bf16[15,128,128]{2,1,0:T(8,128)(2,1)}, /*index=5*/s32[]{:T(128)}) while((s32[]{:T(128)}, bf16[128,128]{1,0:T(8,128)(2,1)S(1)}, f32[15,128,128]{2,1,0:T(8,128)S(1)}, f32[15,128,128]{2,1,0:T(8,128)}, ...), condition=%wide.region_11.12_spmd, body=%wide.region_10.11_spmd.sunk | while | flops 4227074 | bytes 296005 | solution.py:62
  177.3 18.0 %while.64 = (s32[]{:T(128)}, bf16[128,128]{1,0:T(8,128)(2,1)S(1)}, f32[15,128,128]{2,1,0:T(8,128)S(1)}, bf16[15,128,128]{2,1,0:T(8,128)(2,1)}, f32[15,128,128]{2...) while((s32[]{:T(128)}, bf16[128,128]{1,0:T(8,128)(2,1)S(1)}, ...), condition=%wide.region_13.14_spmd, body=%wide.region_12.13_spmd.sunk | while | flops 8437763 | bytes 329825 | solution.py:80
  177.3 1.2 bitcast_dynamic-update-slice_fusion.11
  178.5 1.2 bitcast_dynamic-update-slice_fusion.11
  179.7 1.2 bitcast_dynamic-update-slice_fusion.11
  180.9 1.2 bitcast_dynamic-update-slice_fusion.11
  182.1 1.2 bitcast_dynamic-update-slice_fusion.11
  183.3 1.2 bitcast_dynamic-update-slice_fusion.11
  184.5 1.2 bitcast_dynamic-update-slice_fusion.11
  185.7 1.2 bitcast_dynamic-update-slice_fusion.11
  186.9 1.2 bitcast_dynamic-update-slice_fusion.11
  188.1 1.2 bitcast_dynamic-update-slice_fusion.11
  189.3 1.2 bitcast_dynamic-update-slice_fusion.11
  190.5 1.2 bitcast_dynamic-update-slice_fusion.11
  191.7 1.2 bitcast_dynamic-update-slice_fusion.11
  192.9 1.2 bitcast_dynamic-update-slice_fusion.11
  194.1 1.2 bitcast_dynamic-update-slice_fusion.11
  196.0 1.7 collective-permute-start.13
  197.7 1.8 collective-permute-start.14
  199.5 2.0 collective-permute-start.15
  202.6 2.3 collective-permute-start.16
  204.9 1.1 subtract_divide_fusion.1
  206.0 6.4 %fusion.45 = f32[2048,128]{0,1:T(8,128)S(1)} fusion(bf16[2048,128]{1,0:T(8,128)(2,1)S(1)} %bitcast.327, bf16[1,1,1,2048,2048]{4,3,2,1,0:T(8,128)(2,1)} %param.27), kind=kOutput, calls=%fused_computation.43 | convolution fusion | flops 1073741824 | bytes 9961472 | tf_op jit(solution)/shard_map/dot_general | solution.py:41
  218.7 1.9 copy.18
  221.7 1.3 multiply_reduce_fusion
  222.9 1.3 copy.19
  224.2 1.5 fusion.48
  225.8 38.7 %all-reduce.1 = (f32[2,128]{1,0:T(2,128)S(1)}, f32[128]{0:T(128)S(1)}) all-reduce(f32[2,128]{1,0:T(2,128)S(1)} %fusion.48, f32[128]{0:T(128)S(1)} %get-tuple-element.426), channel_id=1, replica_groups=mesh['gx'=4,'gy'=4,'gz'=2] {'gx','gy','gz'}, use_global_device_ids=true, to_apply=%region_15.16 | all-reduce | flops 384 | bytes 3072 | tf_op jit(solution)/shard_map/psum | solution.py:132
  264.4 1.3 scatter.16
  266.6 2.8 %multiply_add_fusion = f32[1,1,1,2048,128]{4,3,2,1,0:T(8,128)} fusion(f32[1,1,1,2048,128]{4,3,2,1,0:T(8,128)} %bitcast.326, f32[1,1,1,2048,128]{4,3,2,1,0:T(8,128)} %bitcast.325, bf16[1,1,1,2048,128]{4,3,2,1,0:T(8,128)(2,1)} %param.26, f32[128]{0:T(128)S(1)} %get-tuple-element.413, f32[128]{0:T(128)S(1)} %get-tuple-element.412), kind=kLoop, calls=%fused_computation.56 | loop fusion | flops 1310720 | bytes 3671040 | tf_op jit(solution)/shard_map/add | solution.py:145
  (204 shorter events, 53.6 us)
Async XLA Ops:
  0.6 22.2 %copy-start = (bf16[1,1,1,6,128,128]{5,4,3,2,1,0:T(8,128)(2,1)S(1)}, bf16[1,1,1,6,128,128]{5,4,3,2,1,0:T(8,128)(2,1)}, u32[]{:S(2)}) copy-start(bf16[1,1,1,6,128,128]{5,4,3,2,1,0:T(8,128)(2,1)} %param.28) | copy-start | bytes 589828
  0.6 16.4 %copy-start.8 = (bf16[1,1,1,16,128,128]{5,4,3,2,1,0:T(8,128)(2,1)S(1)}, bf16[1,1,1,16,128,128]{5,4,3,2,1,0:T(8,128)(2,1)}, u32[]{:S(2)}) copy-start(bf16[1,1,1,16,128,128]{5,4,3,2,1,0:T(8,128)(2,1)} %param.29) | copy-start | bytes 1572868
  0.7 22.4 %copy-start.4 = (bf16[1,1,1,2048,128]{4,3,2,1,0:T(8,128)(2,1)S(1)}, bf16[1,1,1,2048,128]{4,3,2,1,0:T(8,128)(2,1)}, u32[]{:S(2)}) copy-start(bf16[1,1,1,2048,128]{4,3,2,1,0:T(8,128)(2,1)} %param.25) | copy-start | bytes 1572868
  1.7 16.9 %collective-permute-start = (bf16[1,2,128,128]{3,2,1,0:T(8,128)(2,1)S(1)}, bf16[1,2,128,128]{3,2,1,0:T(8,128)(2,1)S(1)}, u32[]{:S(2)}, u32[]{:S(2)}) collective-permute-start(bf16[1,2,128,128]{3,2,1,0:T(8,128)(2,1)S(1)} %bitcast.342), channel_id=1, source_target_pairs={{0,8},{8,16},{16,24},{24,0},{1,9},{9,17},{17,25},{25,1},{2,10},{10... | collective-permute-start | bytes 196616 | tf_op jit(solution)/shard_map/ppermute | solution.py:22
  2.2 16.6 %collective-permute-start.1 = (bf16[1,2,128,128]{3,2,1,0:T(8,128)(2,1)S(1)}, bf16[1,2,128,128]{3,2,1,0:T(8,128)(2,1)S(1)}, u32[]{:S(2)}, u32[]{:S(2)}) collective-permute-start(bf16[1,2,128,128]{3,2,1,0:T(8,128)(2,1)S(1)} %bitcast.343), channel_id=1, source_target_pairs={{8,0},{16,8},{24,16},{0,24},{9,1},{17,9},{25,17},{1,25},{10,2},{18... | collective-permute-start | bytes 196616 | tf_op jit(solution)/shard_map/ppermute | solution.py:24
  4.2 14.6 %collective-permute-start.2 = (bf16[1,2,128,128]{3,2,1,0:T(8,128)(2,1)S(1)}, bf16[1,2,128,128]{3,2,1,0:T(8,128)(2,1)S(1)}, u32[]{:S(2)}, u32[]{:S(2)}) collective-permute-start(bf16[1,2,128,128]{3,2,1,0:T(8,128)(2,1)S(1)} %bitcast.340), channel_id=1, source_target_pairs={{0,2},{2,4},{4,6},{6,0},{1,3},{3,5},{5,7},{7,1},{8,10},{10,12},{12... | collective-permute-start | bytes 196616 | tf_op jit(solution)/shard_map/ppermute | solution.py:22
  6.5 12.3 %collective-permute-start.3 = (bf16[1,2,128,128]{3,2,1,0:T(8,128)(2,1)S(1)}, bf16[1,2,128,128]{3,2,1,0:T(8,128)(2,1)S(1)}, u32[]{:S(2)}, u32[]{:S(2)}) collective-permute-start(bf16[1,2,128,128]{3,2,1,0:T(8,128)(2,1)S(1)} %bitcast.341), channel_id=1, source_target_pairs={{2,0},{4,2},{6,4},{0,6},{3,1},{5,3},{7,5},{1,7},{10,8},{12,10},{14... | collective-permute-start | bytes 196616 | tf_op jit(solution)/shard_map/ppermute | solution.py:24
  8.6 10.3 %collective-permute-start.4 = (bf16[1,2,128,128]{3,2,1,0:T(8,128)(2,1)S(1)}, bf16[1,2,128,128]{3,2,1,0:T(8,128)(2,1)S(1)}, u32[]{:S(2)}, u32[]{:S(2)}) collective-permute-start(bf16[1,2,128,128]{3,2,1,0:T(8,128)(2,1)S(1)} %bitcast.338), channel_id=1, source_target_pairs={{0,1},{1,0},{2,3},{3,2},{4,5},{5,4},{6,7},{7,6},{8,9},{9,8},{10,11... | collective-permute-start | bytes 196616 | tf_op jit(solution)/shard_map/ppermute | solution.py:22
  18.6 4.3 %collective-permute-start.5 = (bf16[1,2,128,128]{3,2,1,0:T(8,128)(2,1)S(1)}, bf16[1,2,128,128]{3,2,1,0:T(8,128)(2,1)S(1)}, u32[]{:S(2)}, u32[]{:S(2)}) collective-permute-start(bf16[1,2,128,128]{3,2,1,0:T(8,128)(2,1)S(1)} %bitcast.339), channel_id=1, source_target_pairs={{1,0},{0,1},{3,2},{2,3},{5,4},{4,5},{7,6},{6,7},{9,8},{8,9},{11,10... | collective-permute-start | bytes 196616 | tf_op jit(solution)/shard_map/ppermute | solution.py:24
  99.1 15.0 %collective-permute-start.6 = (bf16[1,2,128,128]{3,2,1,0:T(8,128)(2,1)S(1)}, bf16[1,2,128,128]{3,2,1,0:T(8,128)(2,1)S(1)}, u32[]{:S(2)}, u32[]{:S(2)}) collective-permute-start(bf16[1,2,128,128]{3,2,1,0:T(8,128)(2,1)S(1)} %get-tuple-element.441), channel_id=1, source_target_pairs={{0,8},{8,16},{16,24},{24,0},{1,9},{9,17},{17,25},{25,1},{2,10},{10... | collective-permute-start | bytes 196616 | tf_op jit(solution)/shard_map/ppermute | solution.py:22
  99.1 14.9 %collective-permute-start.7 = (bf16[1,2,128,128]{3,2,1,0:T(8,128)(2,1)S(1)}, bf16[1,2,128,128]{3,2,1,0:T(8,128)(2,1)S(1)}, u32[]{:S(2)}, u32[]{:S(2)}) collective-permute-start(bf16[1,2,128,128]{3,2,1,0:T(8,128)(2,1)S(1)} %get-tuple-element.441), channel_id=1, source_target_pairs={{8,0},{16,8},{24,16},{0,24},{9,1},{17,9},{25,17},{1,25},{10,2},{18... | collective-permute-start | bytes 196616 | tf_op jit(solution)/shard_map/ppermute | solution.py:24
  100.9 13.2 %collective-permute-start.8 = (bf16[1,2,128,128]{3,2,1,0:T(8,128)(2,1)S(1)}, bf16[1,2,128,128]{3,2,1,0:T(8,128)(2,1)S(1)}, u32[]{:S(2)}, u32[]{:S(2)}) collective-permute-start(bf16[1,2,128,128]{3,2,1,0:T(8,128)(2,1)S(1)} %get-tuple-element.440), channel_id=1, source_target_pairs={{0,2},{2,4},{4,6},{6,0},{1,3},{3,5},{5,7},{7,1},{8,10},{10,12},{12... | collective-permute-start | bytes 196616 | tf_op jit(solution)/shard_map/ppermute | solution.py:22
  102.8 11.3 %collective-permute-start.9 = (bf16[1,2,128,128]{3,2,1,0:T(8,128)(2,1)S(1)}, bf16[1,2,128,128]{3,2,1,0:T(8,128)(2,1)S(1)}, u32[]{:S(2)}, u32[]{:S(2)}) collective-permute-start(bf16[1,2,128,128]{3,2,1,0:T(8,128)(2,1)S(1)} %get-tuple-element.440), channel_id=1, source_target_pairs={{2,0},{4,2},{6,4},{0,6},{3,1},{5,3},{7,5},{1,7},{10,8},{12,10},{14... | collective-permute-start | bytes 196616 | tf_op jit(solution)/shard_map/ppermute | solution.py:24
  104.7 14.2 %copy-start.5 = (bf16[1,1,1,2048,128]{4,3,2,1,0:T(8,128)(2,1)S(1)}, bf16[1,1,1,2048,128]{4,3,2,1,0:T(8,128)(2,1)}, u32[]{:S(2)}) copy-start(bf16[1,1,1,2048,128]{4,3,2,1,0:T(8,128)(2,1)} %param.25) | copy-start | bytes 1572868
  104.7 14.2 %copy-start.7 = (f32[1,1280,128]{2,1,0:T(8,128)S(1)}, f32[1,1280,128]{2,1,0:T(8,128)}, u32[]{:S(2)}) copy-start(f32[1,1280,128]{2,1,0:T(8,128)} %get-tuple-element.430) | copy-start | bytes 1966084
  110.7 8.2 %copy-start.3 = (f32[1280,128]{1,0:T(8,128)}, f32[1280,128]{1,0:T(8,128)S(1)}, u32[]{:S(2)}) copy-start(f32[1280,128]{1,0:T(8,128)S(1)} %get-tuple-element.433) | copy-start | bytes 1966084
  110.7 8.6 %copy-start.1 = (f32[1,1280,128]{2,1,0:T(8,128)}, f32[1,1280,128]{2,1,0:T(8,128)S(1)}, u32[]{:S(2)}) copy-start(f32[1,1280,128]{2,1,0:T(8,128)S(1)} %get-tuple-element.432) | copy-start | bytes 1966084
  111.8 5.1 %collective-permute-start.10 = (bf16[1,2,128,128]{3,2,1,0:T(8,128)(2,1)S(1)}, bf16[1,2,128,128]{3,2,1,0:T(8,128)(2,1)S(1)}, u32[]{:S(2)}, u32[]{:S(2)}) collective-permute-start(bf16[1,2,128,128]{3,2,1,0:T(8,128)(2,1)S(1)} %get-tuple-element.439), channel_id=1, source_target_pairs={{0,1},{1,0},{2,3},{3,2},{4,5},{5,4},{6,7},{7,6},{8,9},{9,8},{10,11... | collective-permute-start | bytes 196616 | tf_op jit(solution)/shard_map/ppermute | solution.py:22
  114.1 4.3 %collective-permute-start.11 = (bf16[1,2,128,128]{3,2,1,0:T(8,128)(2,1)S(1)}, bf16[1,2,128,128]{3,2,1,0:T(8,128)(2,1)S(1)}, u32[]{:S(2)}, u32[]{:S(2)}) collective-permute-start(bf16[1,2,128,128]{3,2,1,0:T(8,128)(2,1)S(1)} %get-tuple-element.439), channel_id=1, source_target_pairs={{1,0},{0,1},{3,2},{2,3},{5,4},{4,5},{7,6},{6,7},{9,8},{8,9},{11,10... | collective-permute-start | bytes 196616 | tf_op jit(solution)/shard_map/ppermute | solution.py:24
  157.3 47.5 %copy-start.2 = (f32[1,1280,128]{2,1,0:T(8,128)S(1)}, f32[1,1280,128]{2,1,0:T(8,128)}, u32[]{:S(2)}) copy-start(f32[1,1280,128]{2,1,0:T(8,128)} %copy-done.1) | copy-start | bytes 1966084
  196.0 17.4 %collective-permute-start.12 = (bf16[1,2,128,128]{3,2,1,0:T(8,128)(2,1)}, bf16[1,2,128,128]{3,2,1,0:T(8,128)(2,1)}, u32[]{:S(2)}, u32[]{:S(2)}) collective-permute-start(bf16[1,2,128,128]{3,2,1,0:T(8,128)(2,1)} %get-tuple-element.438), channel_id=1, source_target_pairs={{0,8},{8,16},{16,24},{24,0},{1,9},{9,17},{17,25},{25,1},{2,10},{10... | collective-permute-start | bytes 196616 | tf_op jit(solution)/shard_map/ppermute | solution.py:22
  196.0 18.2 %collective-permute-start.13 = (bf16[1,2,128,128]{3,2,1,0:T(8,128)(2,1)}, bf16[1,2,128,128]{3,2,1,0:T(8,128)(2,1)}, u32[]{:S(2)}, u32[]{:S(2)}) collective-permute-start(bf16[1,2,128,128]{3,2,1,0:T(8,128)(2,1)} %get-tuple-element.438), channel_id=1, source_target_pairs={{8,0},{16,8},{24,16},{0,24},{9,1},{17,9},{25,17},{1,25},{10,2},{18... | collective-permute-start | bytes 196616 | tf_op jit(solution)/shard_map/ppermute | solution.py:24
  197.7 17.3 %collective-permute-start.14 = (bf16[1,2,128,128]{3,2,1,0:T(8,128)(2,1)S(1)}, bf16[1,2,128,128]{3,2,1,0:T(8,128)(2,1)}, u32[]{:S(2)}, u32[]{:S(2)}) collective-permute-start(bf16[1,2,128,128]{3,2,1,0:T(8,128)(2,1)S(1)} %get-tuple-element.437), channel_id=1, source_target_pairs={{0,2},{2,4},{4,6},{6,0},{1,3},{3,5},{5,7},{7,1},{8,10},{10,12},{12... | collective-permute-start | bytes 196616 | tf_op jit(solution)/shard_map/ppermute | solution.py:22
  199.5 16.2 %collective-permute-start.15 = (bf16[1,2,128,128]{3,2,1,0:T(8,128)(2,1)S(1)}, bf16[1,2,128,128]{3,2,1,0:T(8,128)(2,1)}, u32[]{:S(2)}, u32[]{:S(2)}) collective-permute-start(bf16[1,2,128,128]{3,2,1,0:T(8,128)(2,1)S(1)} %get-tuple-element.437), channel_id=1, source_target_pairs={{2,0},{4,2},{6,4},{0,6},{3,1},{5,3},{7,5},{1,7},{10,8},{12,10},{14... | collective-permute-start | bytes 196616 | tf_op jit(solution)/shard_map/ppermute | solution.py:24
  202.6 13.9 %collective-permute-start.16 = (bf16[1,2,128,128]{3,2,1,0:T(8,128)(2,1)S(1)}, bf16[1,2,128,128]{3,2,1,0:T(8,128)(2,1)}, u32[]{:S(2)}, u32[]{:S(2)}) collective-permute-start(bf16[1,2,128,128]{3,2,1,0:T(8,128)(2,1)S(1)} %get-tuple-element.436), channel_id=1, source_target_pairs={{0,1},{1,0},{2,3},{3,2},{4,5},{5,4},{6,7},{7,6},{8,9},{9,8},{10,11... | collective-permute-start | bytes 196616 | tf_op jit(solution)/shard_map/ppermute | solution.py:22
  206.0 18.2 %copy-start.6 = (f32[1,2048,128]{2,1,0:T(8,128)S(1)}, f32[1,2048,128]{2,1,0:T(8,128)}, u32[]{:S(2)}) copy-start(f32[1,2048,128]{2,1,0:T(8,128)} %subtract_divide_fusion.1) | copy-start | bytes 3145732
  212.4 53.5 %copy-start.9 = (f32[3]{0:T(128)S(1)}, f32[3]{0:T(128)}, u32[]{:S(2)}) copy-start(f32[3]{0:T(128)} %constant.255.clone.1) | copy-start | bytes 40
  213.4 4.3 %collective-permute-start.17 = (bf16[1,2,128,128]{3,2,1,0:T(8,128)(2,1)S(1)}, bf16[1,2,128,128]{3,2,1,0:T(8,128)(2,1)S(1)}, u32[]{:S(2)}, u32[]{:S(2)}) collective-permute-start(bf16[1,2,128,128]{3,2,1,0:T(8,128)(2,1)S(1)} %get-tuple-element.436), channel_id=1, source_target_pairs={{1,0},{0,1},{3,2},{2,3},{5,4},{4,5},{7,6},{6,7},{9,8},{8,9},{11,10... | collective-permute-start | bytes 196616 | tf_op jit(solution)/shard_map/ppermute | solution.py:24
where the time goes:
time: 273 us; the launch traced here: 269 us
  blocking collectives  115 us (42%)
  matrix products  86.2 us (32%)
  starting transfers between devices  24.7 us (9%)
  local copies, waits for them, and re-layouts  16.3 us (6%)
  other arithmetic  16.3 us (6%)
  waiting for transfers between devices  8.5 us (3%)
    psum x2, blocking collectives, body(): lax.psum((own_products, jnp.sum(mapped * mapped, axis=0)), ('gx', 'gy', '...  76.8 us
    psum x1, blocking collectives, body(): lax.psum(jnp.sum(residual * residual, axis=0), ('gx', 'gy', 'gz')) + epsilon  37.7 us
    dot_general x30, matrix products, backward(): jnp.dot(diag_block, inner.astype(jnp.bfloat16), preferred_element_type=jn...  34.9 us
    dot_general x30, matrix products, forward(): jnp.dot(lower_block, previous.astype(jnp.bfloat16), preferred_element_typ...  30.1 us
    dot_general x3, matrix products, operate(): own_part = jnp.dot(schur_block, values, preferred_element_type=jnp.float32)  18.1 us
    ppermute x9, starting transfers between devices, with_halo(): lax.ppermute(tail, axis, [(i, (i + 1) % count) for i in range(count)])  13 us
    ppermute x9, starting transfers between devices, with_halo(): lax.ppermute(head, axis, [((i + 1) % count, i) for i in range(count)])  11.7 us
    ppermute x9, waiting for transfers between devices, with_halo(): lax.ppermute(head, axis, [((i + 1) % count, i) for i in range(count)])  5.72 us
  transfers between devices with their start and end apart: 18, of which 4 were waited for; matrix products, arithmetic and copies ran while one was open for 11% of the time, Pallas kernels for 0%

commit v1 on v0

--- a/solution.py
+++ b/solution.py
@@ -118,7 +118,8 @@
     warm_start = start_guess[0, 0, 0]
     residual = loads[0, 0, 0].astype(jnp.float32) - operate(warm_start, schur_block, couple_block)
     start_norm = jnp.sqrt(
-        lax.psum(jnp.sum(residual * residual, axis=0), ("gx", "gy", "gz")) + epsilon
+        jnp.sum(lax.all_gather(jnp.sum(residual * residual, axis=0), ("gx", "gy", "gz")), axis=0)
+        + epsilon
     )
     krylov = [residual / start_norm]
     hessenberg = jnp.zeros((ITERS + 1, ITERS, R), jnp.float32)

time: 273 us -> 299 us (1.095)
  blocking collectives: 115 us -> 140 us
    all_gather x0 -> x1, blocking collectives: none -> 63.6 us  [body(): lax.all_gather(jnp.sum(residual * residual, axis=0), ('gx', 'gy', 'gz'))]
    psum x1 -> x0, blocking collectives: 37.7 us -> none  [body(): lax.psum(jnp.sum(residual * residual, axis=0), ('gx', 'gy', 'gz')) + epsilon]
  transfers between devices with their start and end apart: 18 -> 18, of which waited for: 4 -> 4; matrix products, arithmetic and copies ran while one was open for 11% -> 10% of each run, Pallas kernels for 0% -> 0%
where the time goes in v1:
time: 299 us; the launch traced here: 295 us
  blocking collectives  140 us (47%)
  matrix products  86.2 us (29%)
  starting transfers between devices  24.5 us (8%)
  local copies, waits for them, and re-layouts  16.5 us (6%)
  other arithmetic  16.4 us (5%)
  waiting for transfers between devices  8.5 us (3%)
    psum x2, blocking collectives, body(): lax.psum((own_products, jnp.sum(mapped * mapped, axis=0)), ('gx', 'gy', '...  76.7 us
    all_gather x1, blocking collectives, body(): lax.all_gather(jnp.sum(residual * residual, axis=0), ('gx', 'gy', 'gz'))  63.6 us
    dot_general x30, matrix products, backward(): jnp.dot(diag_block, inner.astype(jnp.bfloat16), preferred_element_type=jn...  34.9 us
    dot_general x30, matrix products, forward(): jnp.dot(lower_block, previous.astype(jnp.bfloat16), preferred_element_typ...  30.1 us
    dot_general x3, matrix products, operate(): own_part = jnp.dot(schur_block, values, preferred_element_type=jnp.float32)  18.1 us
    ppermute x9, starting transfers between devices, with_halo(): lax.ppermute(head, axis, [((i + 1) % count, i) for i in range(count)])  12.6 us
    ppermute x9, starting transfers between devices, with_halo(): lax.ppermute(tail, axis, [(i, (i + 1) % count) for i in range(count)])  11.8 us
  transfers between devices with their start and end apart: 18, of which 4 were waited for; matrix products, arithmetic and copies ran while one was open for 10% of the time, Pallas kernels for 0%

profile of v1, /device:TPU:0, one launch (start us, length us, event | category | flops | bytes accessed | tf_op | source)
XLA Modules:
  0.0 295.2 jit_solution(2482972090971689059)
XLA Ops:
  2.2 2.0 collective-permute-start.1
  4.2 2.3 collective-permute-start.2
  6.5 2.0 collective-permute-start.3
  8.6 1.7 collective-permute-start.4
  10.3 5.8 %fusion.40 = f32[2048,128]{1,0:T(8,128)S(1)} fusion(bf16[1,1,1,2048,2048]{4,3,2,1,0:T(8,128)(2,1)} %param.27, bf16[1,1,1,2048,128]{4,3,2,1,0:T(8,128)(2,1)} %param.26), kind=kOutput, calls=%fused_computation.40 | convolution fusion | flops 1073741824 | bytes 9961472 | tf_op jit(solution)/shard_map/dot_general | solution.py:41
  18.9 3.9 %collective-permute-done.5 = bf16[1,2,128,128]{3,2,1,0:T(8,128)(2,1)S(1)} collective-permute-done((bf16[1,2,128,128]{3,2,1,0:T(8,128)(2,1)S(1)}, bf16[1,2,128,128]{3,2,1,0:T(8,128)(2,1)S(1)}, u32[]{:S(2)}, u32[]{:S(2)}) %collective-permute-start.5) | collective-permute-done | bytes 65568 | tf_op jit(solution)/shard_map/ppermute | solution.py:24
  23.4 63.6 %all-gather.1 = f32[32,1,128]{2,1,0:T(1,128)S(1)} all-gather(f32[1,1,128]{2,1,0:T(1,128)S(1)} %bitcast.364), channel_id=2, replica_groups=mesh['gx'=4,'gy'=4,'gz'=2] {'gx','gy','gz'}, dimensions={0}, use_global_device_ids=true | all-gather | bytes 16896 | tf_op jit(solution)/shard_map/all_gather | solution.py:121
  87.1 1.2 fusion.52
  89.4 15.6 %while.61 = (s32[]{:T(128)}, bf16[128,128]{1,0:T(8,128)(2,1)S(1)}, f32[15,128,128]{2,1,0:T(8,128)S(1)}, f32[15,128,128]{2,1,0:T(8,128)}, bf16[15,128,128]{2,1,0:T(8,128)(2,1)}, /*index=5*/s32[]{:T(128)}) while((s32[]{:T(128)}, bf16[128,128]{1,0:T(8,128)(2,1)S(1)}, f32[15,128,128]{2,1,0:T(8,128)S(1)}, f32[15,128,128]{2,1,0:T(8,128)}, ...), condition=%wide.region_3.4_spmd, body=%wide.region_2.3_spmd.sunk | while | flops 4227074 | bytes 296005 | solution.py:62
  107.0 18.0 %while.62 = (s32[]{:T(128)}, bf16[128,128]{1,0:T(8,128)(2,1)S(1)}, f32[15,128,128]{2,1,0:T(8,128)S(1)}, bf16[15,128,128]{2,1,0:T(8,128)(2,1)}, f32[15,128,128]{2...) while((s32[]{:T(128)}, bf16[128,128]{1,0:T(8,128)(2,1)S(1)}, ...), condition=%wide.region_5.6_spmd, body=%wide.region_4.5_spmd.sunk | while | flops 8437763 | bytes 329825 | solution.py:80
  107.0 1.2 bitcast_dynamic-update-slice_fusion.9
  108.2 1.2 bitcast_dynamic-update-slice_fusion.9
  109.4 1.2 bitcast_dynamic-update-slice_fusion.9
  110.6 1.2 bitcast_dynamic-update-slice_fusion.9
  111.8 1.2 bitcast_dynamic-update-slice_fusion.9
  113.0 1.2 bitcast_dynamic-update-slice_fusion.9
  114.2 1.2 bitcast_dynamic-update-slice_fusion.9
  115.4 1.2 bitcast_dynamic-update-slice_fusion.9
  116.6 1.2 bitcast_dynamic-update-slice_fusion.9
  117.8 1.2 bitcast_dynamic-update-slice_fusion.9
  119.0 1.2 bitcast_dynamic-update-slice_fusion.9
  120.2 1.2 bitcast_dynamic-update-slice_fusion.9
  121.4 1.2 bitcast_dynamic-update-slice_fusion.9
  122.6 1.2 bitcast_dynamic-update-slice_fusion.9
  123.8 1.2 bitcast_dynamic-update-slice_fusion.9
  125.1 1.7 collective-permute-start.7
  126.8 3.8 %collective-permute-start.9 = (bf16[1,2,128,128]{3,2,1,0:T(8,128)(2,1)S(1)}, bf16[1,2,128,128]{3,2,1,0:T(8,128)(2,1)S(1)}, u32[]{:S(2)}, u32[]{:S(2)}) collective-permute-start(bf16[1,2,128,128]{3,2,1,0:T(8,128)(2,1)S(1)} %get-tuple-element.440), channel_id=1, source_target_pairs={{2,0},{4,2},{6,4},{0,6},{3,1},{5,3},{7,5},{1,7},{10,8},{12,10},{14... | collective-permute-start | bytes 196616 | tf_op jit(solution)/shard_map/ppermute | solution.py:24
  130.7 5.9 %fusion.42 = f32[2048,128]{1,0:T(8,128)S(1)} fusion(bf16[2048,128]{1,0:T(8,128)(2,1)S(1)} %bitcast.349, bf16[1,1,1,2048,2048]{4,3,2,1,0:T(8,128)(2,1)} %param.27), kind=kOutput, calls=%fused_computation.42 | convolution fusion | flops 1073741824 | bytes 9961472 | tf_op jit(solution)/shard_map/dot_general | solution.py:41
  136.6 1.1 pad_maximum_fusion
  137.8 2.0 collective-permute-start.10
  139.9 2.7 collective-permute-done.10
  142.6 1.5 collective-permute-done.11
  145.0 37.0 %all-reduce.2 = (f32[128]{0:T(128)S(1)}, f32[1,128]{1,0:T(1,128)S(1)}) all-reduce(f32[128]{0:T(128)S(1)} %multiply_reduce_fusion.1, f32[1,128]{1,0:T(1,128)S(1)} %bitcast.366), channel_id=1, replica_groups=mesh['gx'=4,'gy'=4,'gz'=2] {'gx','gy','gz'}, use_global_device_ids=true, to_apply=%region_9.10 | all-reduce | flops 256 | bytes 2048 | tf_op jit(solution)/shard_map/psum | solution.py:133
  182.0 1.3 subtract_divide_fusion
  184.4 15.6 %while.63 = (s32[]{:T(128)}, bf16[128,128]{1,0:T(8,128)(2,1)S(1)}, f32[15,128,128]{2,1,0:T(8,128)S(1)}, f32[15,128,128]{2,1,0:T(8,128)}, bf16[15,128,128]{2,1,0:T(8,128)(2,1)}, /*index=5*/s32[]{:T(128)}) while((s32[]{:T(128)}, bf16[128,128]{1,0:T(8,128)(2,1)S(1)}, f32[15,128,128]{2,1,0:T(8,128)S(1)}, f32[15,128,128]{2,1,0:T(8,128)}, ...), condition=%wide.region_11.12_spmd, body=%wide.region_10.11_spmd.sunk | while | flops 4227074 | bytes 296005 | solution.py:62
  202.0 18.0 %while.64 = (s32[]{:T(128)}, bf16[128,128]{1,0:T(8,128)(2,1)S(1)}, f32[15,128,128]{2,1,0:T(8,128)S(1)}, bf16[15,128,128]{2,1,0:T(8,128)(2,1)}, f32[15,128,128]{2...) while((s32[]{:T(128)}, bf16[128,128]{1,0:T(8,128)(2,1)S(1)}, ...), condition=%wide.region_13.14_spmd, body=%wide.region_12.13_spmd.sunk | while | flops 8437763 | bytes 329825 | solution.py:80
  202.0 1.2 bitcast_dynamic-update-slice_fusion.11
  203.2 1.2 bitcast_dynamic-update-slice_fusion.11
  204.4 1.2 bitcast_dynamic-update-slice_fusion.11
  205.6 1.2 bitcast_dynamic-update-slice_fusion.11
  206.8 1.2 bitcast_dynamic-update-slice_fusion.11
  208.0 1.2 bitcast_dynamic-update-slice_fusion.11
  209.2 1.2 bitcast_dynamic-update-slice_fusion.11
  210.4 1.2 bitcast_dynamic-update-slice_fusion.11
  211.6 1.2 bitcast_dynamic-update-slice_fusion.11
  212.8 1.2 bitcast_dynamic-update-slice_fusion.11
  214.0 1.2 bitcast_dynamic-update-slice_fusion.11
  215.2 1.2 bitcast_dynamic-update-slice_fusion.11
  216.4 1.2 bitcast_dynamic-update-slice_fusion.11
  217.6 1.2 bitcast_dynamic-update-slice_fusion.11
  218.8 1.2 bitcast_dynamic-update-slice_fusion.11
  220.7 1.7 collective-permute-start.13
  222.4 2.9 collective-permute-start.14
  226.2 1.0 pad_maximum_fusion.3
  227.3 2.3 collective-permute-start.16
  229.6 1.1 subtract_divide_fusion.1
  230.7 6.4 %fusion.45 = f32[2048,128]{0,1:T(8,128)S(1)} fusion(bf16[2048,128]{1,0:T(8,128)(2,1)S(1)} %bitcast.341, bf16[1,1,1,2048,2048]{4,3,2,1,0:T(8,128)(2,1)} %param.27), kind=kOutput, calls=%fused_computation.43 | convolution fusion | flops 1073741824 | bytes 9961472 | tf_op jit(solution)/shard_map/dot_general | solution.py:41
  243.4 1.9 copy.30
  246.3 1.3 multiply_reduce_fusion
  247.6 1.3 copy.31
  248.9 1.5 fusion.48
  250.4 39.7 %all-reduce.1 = (f32[2,128]{1,0:T(2,128)S(1)}, f32[128]{0:T(128)S(1)}) all-reduce(f32[2,128]{1,0:T(2,128)S(1)} %fusion.48, f32[128]{0:T(128)S(1)} %get-tuple-element.426), channel_id=1, replica_groups=mesh['gx'=4,'gy'=4,'gz'=2] {'gx','gy','gz'}, use_global_device_ids=true, to_apply=%region_15.16 | all-reduce | flops 384 | bytes 3072 | tf_op jit(solution)/shard_map/psum | solution.py:133
  290.1 1.4 scatter.16
  292.4 2.8 multiply_add_fusion
  (204 shorter events, 52.5 us)
Async XLA Ops:
  0.6 22.2 %copy-start = (bf16[1,1,1,6,128,128]{5,4,3,2,1,0:T(8,128)(2,1)S(1)}, bf16[1,1,1,6,128,128]{5,4,3,2,1,0:T(8,128)(2,1)}, u32[]{:S(2)}) copy-start(bf16[1,1,1,6,128,128]{5,4,3,2,1,0:T(8,128)(2,1)} %param.28) | copy-start | bytes 589828
  0.6 16.4 %copy-start.8 = (bf16[1,1,1,16,128,128]{5,4,3,2,1,0:T(8,128)(2,1)S(1)}, bf16[1,1,1,16,128,128]{5,4,3,2,1,0:T(8,128)(2,1)}, u32[]{:S(2)}) copy-start(bf16[1,1,1,16,128,128]{5,4,3,2,1,0:T(8,128)(2,1)} %param.29) | copy-start | bytes 1572868
  0.7 22.5 %copy-start.4 = (bf16[1,1,1,2048,128]{4,3,2,1,0:T(8,128)(2,1)S(1)}, bf16[1,1,1,2048,128]{4,3,2,1,0:T(8,128)(2,1)}, u32[]{:S(2)}) copy-start(bf16[1,1,1,2048,128]{4,3,2,1,0:T(8,128)(2,1)} %param.25) | copy-start | bytes 1572868
  1.7 16.9 %collective-permute-start = (bf16[1,2,128,128]{3,2,1,0:T(8,128)(2,1)S(1)}, bf16[1,2,128,128]{3,2,1,0:T(8,128)(2,1)S(1)}, u32[]{:S(2)}, u32[]{:S(2)}) collective-permute-start(bf16[1,2,128,128]{3,2,1,0:T(8,128)(2,1)S(1)} %bitcast.356), channel_id=1, source_target_pairs={{0,8},{8,16},{16,24},{24,0},{1,9},{9,17},{17,25},{25,1},{2,10},{10... | collective-permute-start | bytes 196616 | tf_op jit(solution)/shard_map/ppermute | solution.py:22
  2.2 16.6 %collective-permute-start.1 = (bf16[1,2,128,128]{3,2,1,0:T(8,128)(2,1)S(1)}, bf16[1,2,128,128]{3,2,1,0:T(8,128)(2,1)S(1)}, u32[]{:S(2)}, u32[]{:S(2)}) collective-permute-start(bf16[1,2,128,128]{3,2,1,0:T(8,128)(2,1)S(1)} %bitcast.357), channel_id=1, source_target_pairs={{8,0},{16,8},{24,16},{0,24},{9,1},{17,9},{25,17},{1,25},{10,2},{18... | collective-permute-start | bytes 196616 | tf_op jit(solution)/shard_map/ppermute | solution.py:24
  4.2 14.7 %collective-permute-start.2 = (bf16[1,2,128,128]{3,2,1,0:T(8,128)(2,1)S(1)}, bf16[1,2,128,128]{3,2,1,0:T(8,128)(2,1)S(1)}, u32[]{:S(2)}, u32[]{:S(2)}) collective-permute-start(bf16[1,2,128,128]{3,2,1,0:T(8,128)(2,1)S(1)} %bitcast.354), channel_id=1, source_target_pairs={{0,2},{2,4},{4,6},{6,0},{1,3},{3,5},{5,7},{7,1},{8,10},{10,12},{12... | collective-permute-start | bytes 196616 | tf_op jit(solution)/shard_map/ppermute | solution.py:22
  6.5 12.4 %collective-permute-start.3 = (bf16[1,2,128,128]{3,2,1,0:T(8,128)(2,1)S(1)}, bf16[1,2,128,128]{3,2,1,0:T(8,128)(2,1)S(1)}, u32[]{:S(2)}, u32[]{:S(2)}) collective-permute-start(bf16[1,2,128,128]{3,2,1,0:T(8,128)(2,1)S(1)} %bitcast.355), channel_id=1, source_target_pairs={{2,0},{4,2},{6,4},{0,6},{3,1},{5,3},{7,5},{1,7},{10,8},{12,10},{14... | collective-permute-start | bytes 196616 | tf_op jit(solution)/shard_map/ppermute | solution.py:24
  8.6 10.4 %collective-permute-start.4 = (bf16[1,2,128,128]{3,2,1,0:T(8,128)(2,1)S(1)}, bf16[1,2,128,128]{3,2,1,0:T(8,128)(2,1)S(1)}, u32[]{:S(2)}, u32[]{:S(2)}) collective-permute-start(bf16[1,2,128,128]{3,2,1,0:T(8,128)(2,1)S(1)} %bitcast.352), channel_id=1, source_target_pairs={{0,1},{1,0},{2,3},{3,2},{4,5},{5,4},{6,7},{7,6},{8,9},{9,8},{10,11... | collective-permute-start | bytes 196616 | tf_op jit(solution)/shard_map/ppermute | solution.py:22
  18.6 4.3 %collective-permute-start.5 = (bf16[1,2,128,128]{3,2,1,0:T(8,128)(2,1)S(1)}, bf16[1,2,128,128]{3,2,1,0:T(8,128)(2,1)S(1)}, u32[]{:S(2)}, u32[]{:S(2)}) collective-permute-start(bf16[1,2,128,128]{3,2,1,0:T(8,128)(2,1)S(1)} %bitcast.353), channel_id=1, source_target_pairs={{1,0},{0,1},{3,2},{2,3},{5,4},{4,5},{7,6},{6,7},{9,8},{8,9},{11,10... | collective-permute-start | bytes 196616 | tf_op jit(solution)/shard_map/ppermute | solution.py:24
  125.0 14.8 %collective-permute-start.6 = (bf16[1,2,128,128]{3,2,1,0:T(8,128)(2,1)S(1)}, bf16[1,2,128,128]{3,2,1,0:T(8,128)(2,1)S(1)}, u32[]{:S(2)}, u32[]{:S(2)}) collective-permute-start(bf16[1,2,128,128]{3,2,1,0:T(8,128)(2,1)S(1)} %get-tuple-element.441), channel_id=1, source_target_pairs={{0,8},{8,16},{16,24},{24,0},{1,9},{9,17},{17,25},{25,1},{2,10},{10... | collective-permute-start | bytes 196616 | tf_op jit(solution)/shard_map/ppermute | solution.py:22
  125.1 14.7 %collective-permute-start.7 = (bf16[1,2,128,128]{3,2,1,0:T(8,128)(2,1)S(1)}, bf16[1,2,128,128]{3,2,1,0:T(8,128)(2,1)S(1)}, u32[]{:S(2)}, u32[]{:S(2)}) collective-permute-start(bf16[1,2,128,128]{3,2,1,0:T(8,128)(2,1)S(1)} %get-tuple-element.441), channel_id=1, source_target_pairs={{8,0},{16,8},{24,16},{0,24},{9,1},{17,9},{25,17},{1,25},{10,2},{18... | collective-permute-start | bytes 196616 | tf_op jit(solution)/shard_map/ppermute | solution.py:24
  126.8 13.0 %collective-permute-start.8 = (bf16[1,2,128,128]{3,2,1,0:T(8,128)(2,1)S(1)}, bf16[1,2,128,128]{3,2,1,0:T(8,128)(2,1)S(1)}, u32[]{:S(2)}, u32[]{:S(2)}) collective-permute-start(bf16[1,2,128,128]{3,2,1,0:T(8,128)(2,1)S(1)} %get-tuple-element.440), channel_id=1, source_target_pairs={{0,2},{2,4},{4,6},{6,0},{1,3},{3,5},{5,7},{7,1},{8,10},{10,12},{12... | collective-permute-start | bytes 196616 | tf_op jit(solution)/shard_map/ppermute | solution.py:22
  126.8 13.0 %collective-permute-start.9 = (bf16[1,2,128,128]{3,2,1,0:T(8,128)(2,1)S(1)}, bf16[1,2,128,128]{3,2,1,0:T(8,128)(2,1)S(1)}, u32[]{:S(2)}, u32[]{:S(2)}) collective-permute-start(bf16[1,2,128,128]{3,2,1,0:T(8,128)(2,1)S(1)} %get-tuple-element.440), channel_id=1, source_target_pairs={{2,0},{4,2},{6,4},{0,6},{3,1},{5,3},{7,5},{1,7},{10,8},{12,10},{14... | collective-permute-start | bytes 196616 | tf_op jit(solution)/shard_map/ppermute | solution.py:24
  130.7 14.0 %copy-start.5 = (bf16[1,1,1,2048,128]{4,3,2,1,0:T(8,128)(2,1)S(1)}, bf16[1,1,1,2048,128]{4,3,2,1,0:T(8,128)(2,1)}, u32[]{:S(2)}) copy-start(bf16[1,1,1,2048,128]{4,3,2,1,0:T(8,128)(2,1)} %param.25) | copy-start | bytes 1572868
  130.7 14.0 %copy-start.7 = (f32[1,1280,128]{2,1,0:T(8,128)S(1)}, f32[1,1280,128]{2,1,0:T(8,128)}, u32[]{:S(2)}) copy-start(f32[1,1280,128]{2,1,0:T(8,128)} %get-tuple-element.430) | copy-start | bytes 1966084
  136.6 8.0 %copy-start.3 = (f32[1280,128]{1,0:T(8,128)}, f32[1280,128]{1,0:T(8,128)S(1)}, u32[]{:S(2)}) copy-start(f32[1280,128]{1,0:T(8,128)S(1)} %get-tuple-element.433) | copy-start | bytes 1966084
  136.6 8.3 %copy-start.1 = (f32[1,1280,128]{2,1,0:T(8,128)}, f32[1,1280,128]{2,1,0:T(8,128)S(1)}, u32[]{:S(2)}) copy-start(f32[1,1280,128]{2,1,0:T(8,128)S(1)} %get-tuple-element.432) | copy-start | bytes 1966084
  137.8 4.8 %collective-permute-start.10 = (bf16[1,2,128,128]{3,2,1,0:T(8,128)(2,1)S(1)}, bf16[1,2,128,128]{3,2,1,0:T(8,128)(2,1)S(1)}, u32[]{:S(2)}, u32[]{:S(2)}) collective-permute-start(bf16[1,2,128,128]{3,2,1,0:T(8,128)(2,1)S(1)} %get-tuple-element.439), channel_id=1, source_target_pairs={{0,1},{1,0},{2,3},{3,2},{4,5},{5,4},{6,7},{7,6},{8,9},{9,8},{10,11... | collective-permute-start | bytes 196616 | tf_op jit(solution)/shard_map/ppermute | solution.py:22
  139.8 4.3 %collective-permute-start.11 = (bf16[1,2,128,128]{3,2,1,0:T(8,128)(2,1)S(1)}, bf16[1,2,128,128]{3,2,1,0:T(8,128)(2,1)S(1)}, u32[]{:S(2)}, u32[]{:S(2)}) collective-permute-start(bf16[1,2,128,128]{3,2,1,0:T(8,128)(2,1)S(1)} %get-tuple-element.439), channel_id=1, source_target_pairs={{1,0},{0,1},{3,2},{2,3},{5,4},{4,5},{7,6},{6,7},{9,8},{8,9},{11,10... | collective-permute-start | bytes 196616 | tf_op jit(solution)/shard_map/ppermute | solution.py:24
  182.0 47.5 %copy-start.2 = (f32[1,1280,128]{2,1,0:T(8,128)S(1)}, f32[1,1280,128]{2,1,0:T(8,128)}, u32[]{:S(2)}) copy-start(f32[1,1280,128]{2,1,0:T(8,128)} %copy-done.1) | copy-start | bytes 1966084
  220.7 17.4 %collective-permute-start.12 = (bf16[1,2,128,128]{3,2,1,0:T(8,128)(2,1)}, bf16[1,2,128,128]{3,2,1,0:T(8,128)(2,1)}, u32[]{:S(2)}, u32[]{:S(2)}) collective-permute-start(bf16[1,2,128,128]{3,2,1,0:T(8,128)(2,1)} %get-tuple-element.438), channel_id=1, source_target_pairs={{0,8},{8,16},{16,24},{24,0},{1,9},{9,17},{17,25},{25,1},{2,10},{10... | collective-permute-start | bytes 196616 | tf_op jit(solution)/shard_map/ppermute | solution.py:22
  220.7 18.3 %collective-permute-start.13 = (bf16[1,2,128,128]{3,2,1,0:T(8,128)(2,1)}, bf16[1,2,128,128]{3,2,1,0:T(8,128)(2,1)}, u32[]{:S(2)}, u32[]{:S(2)}) collective-permute-start(bf16[1,2,128,128]{3,2,1,0:T(8,128)(2,1)} %get-tuple-element.438), channel_id=1, source_target_pairs={{8,0},{16,8},{24,16},{0,24},{9,1},{17,9},{25,17},{1,25},{10,2},{18... | collective-permute-start | bytes 196616 | tf_op jit(solution)/shard_map/ppermute | solution.py:24
  222.4 17.3 %collective-permute-start.14 = (bf16[1,2,128,128]{3,2,1,0:T(8,128)(2,1)S(1)}, bf16[1,2,128,128]{3,2,1,0:T(8,128)(2,1)}, u32[]{:S(2)}, u32[]{:S(2)}) collective-permute-start(bf16[1,2,128,128]{3,2,1,0:T(8,128)(2,1)S(1)} %get-tuple-element.437), channel_id=1, source_target_pairs={{0,2},{2,4},{4,6},{6,0},{1,3},{3,5},{5,7},{7,1},{8,10},{10,12},{12... | collective-permute-start | bytes 196616 | tf_op jit(solution)/shard_map/ppermute | solution.py:22
  225.3 15.2 %collective-permute-start.15 = (bf16[1,2,128,128]{3,2,1,0:T(8,128)(2,1)S(1)}, bf16[1,2,128,128]{3,2,1,0:T(8,128)(2,1)}, u32[]{:S(2)}, u32[]{:S(2)}) collective-permute-start(bf16[1,2,128,128]{3,2,1,0:T(8,128)(2,1)S(1)} %get-tuple-element.437), channel_id=1, source_target_pairs={{2,0},{4,2},{6,4},{0,6},{3,1},{5,3},{7,5},{1,7},{10,8},{12,10},{14... | collective-permute-start | bytes 196616 | tf_op jit(solution)/shard_map/ppermute | solution.py:24
  227.3 14.0 %collective-permute-start.16 = (bf16[1,2,128,128]{3,2,1,0:T(8,128)(2,1)S(1)}, bf16[1,2,128,128]{3,2,1,0:T(8,128)(2,1)}, u32[]{:S(2)}, u32[]{:S(2)}) collective-permute-start(bf16[1,2,128,128]{3,2,1,0:T(8,128)(2,1)S(1)} %get-tuple-element.436), channel_id=1, source_target_pairs={{0,1},{1,0},{2,3},{3,2},{4,5},{5,4},{6,7},{7,6},{8,9},{9,8},{10,11... | collective-permute-start | bytes 196616 | tf_op jit(solution)/shard_map/ppermute | solution.py:22
  230.7 18.2 %copy-start.6 = (f32[1,2048,128]{2,1,0:T(8,128)S(1)}, f32[1,2048,128]{2,1,0:T(8,128)}, u32[]{:S(2)}) copy-start(f32[1,2048,128]{2,1,0:T(8,128)} %subtract_divide_fusion.1) | copy-start | bytes 3145732
  237.1 54.6 %copy-start.9 = (f32[3]{0:T(128)S(1)}, f32[3]{0:T(128)}, u32[]{:S(2)}) copy-start(f32[3]{0:T(128)} %constant.255.clone.1) | copy-start | bytes 40
  238.1 4.3 %collective-permute-start.17 = (bf16[1,2,128,128]{3,2,1,0:T(8,128)(2,1)S(1)}, bf16[1,2,128,128]{3,2,1,0:T(8,128)(2,1)S(1)}, u32[]{:S(2)}, u32[]{:S(2)}) collective-permute-start(bf16[1,2,128,128]{3,2,1,0:T(8,128)(2,1)S(1)} %get-tuple-element.436), channel_id=1, source_target_pairs={{1,0},{0,1},{3,2},{2,3},{5,4},{4,5},{7,6},{6,7},{9,8},{8,9},{11,10... | collective-permute-start | bytes 196616 | tf_op jit(solution)/shard_map/ppermute | solution.py:24
